TPU v7x, 32 devices: a whole 2x2x4 slice. The times are simulated.
32 devices in a mesh: feat: 16 (over z, y, x), rows: 2 (over core).
Axes of the slice: x: 2, y: 2, z: 4, core: 2. Of those that a mesh axis runs over, the one named last changes fastest.
Arguments:
- grads: bfloat16 [16384], P(('rows', 'feat')), may hold values from -6 to 6
- hessians: bfloat16 [16384], P(('rows', 'feat')), may hold values from 0.019897461 to 0.25
- nodes: int32 [16384], P(('rows', 'feat')), may hold values from 0 to 15
- bins: int32 [512, 16384], P('feat', 'rows'), may hold values from 0 to 255
Outputs:
- histogram: float32 [2, 16, 512, 256], P(None, 'rows', 'feat')
- best_gain: float32 [16], P('rows')
All inputs are finite; a program needn't handle non-finite values.
Results may differ from a plain program's by a relative error of at most 0.0003.
Values may be sent and summed in bfloat16 or wider, within the bound.
A program may use at most 64 MiB of HBM per device.

v0:
```python
import jax
import jax.numpy as jnp
from jax import lax
from jax.sharding import PartitionSpec as P

BINS = 256
NODES = 16


reg_lambda = 1.0
block_rows = 512


def split_gain(hist):
    left_g = jnp.cumsum(hist[0], axis=-1)
    left_h = jnp.cumsum(hist[1], axis=-1)
    total_g = left_g[..., -1:]
    total_h = left_h[..., -1:]
    gain = left_g * left_g / (left_h + reg_lambda)
    gain = gain + (total_g - left_g) ** 2 / (total_h - left_h + reg_lambda)
    gain = gain - total_g * total_g / (total_h + reg_lambda)
    return jnp.max(gain, axis=(1, 2))


def make_panel(grads, hessians, nodes):
    node_ids = lax.broadcasted_iota(jnp.int32, (NODES, nodes.shape[0]), 0)
    node_hot = (nodes[None, :] == node_ids).astype(jnp.bfloat16)
    return jnp.concatenate([grads[None, :] * node_hot, hessians[None, :] * node_hot], axis=0)


def add_block(hist, bins_block, panel_block):
    count = panel_block.shape[1]
    bin_ids = lax.broadcasted_iota(jnp.int32, (1, BINS, 1), 1)
    one_hot = (bins_block[:, None, :] == bin_ids).astype(jnp.bfloat16).reshape(-1, count)
    return hist + lax.dot_general(
        panel_block, one_hot, (((1,), (1,)), ((), ())), preferred_element_type=jnp.float32
    )


def accumulate(hist, bins_part, panel_part):
    count = panel_part.shape[1]

    def step(which, carry):
        begin = which * block_rows
        bins_block = lax.dynamic_slice_in_dim(bins_part, begin, block_rows, 1)
        panel_block = lax.dynamic_slice_in_dim(panel_part, begin, block_rows, 1)
        return add_block(carry, bins_block, panel_block)

    return lax.fori_loop(0, count // block_rows, step, hist)


def local(grads, hessians, nodes, bins):
    feat_dev = bins.shape[0]
    empty = jnp.zeros((2 * NODES, feat_dev * BINS), jnp.float32)
    local_panel = make_panel(grads, hessians, nodes)
    hist = accumulate(empty, bins, lax.all_gather(local_panel, "feat", axis=1, tiled=True))
    hist = hist.reshape(2, NODES, feat_dev, BINS)
    share = NODES // lax.axis_size("rows")
    total = lax.psum(hist, "rows")
    mine = lax.dynamic_slice_in_dim(total, lax.axis_index("rows") * share, share, 1)
    best = lax.pmax(split_gain(mine), "feat")
    return (mine, best)


def solution(mesh):
    return jax.shard_map(
        local,
        mesh=mesh,
        in_specs=(P(("rows", "feat")), P(("rows", "feat")), P(("rows", "feat")), P("feat", "rows")),
        out_specs=(P(None, "rows", "feat", None), P("rows")),
        check_vma=False,
    )
```

profile of v0, /device:TPU:0, one launch (start us, length us, event | category | flops | bytes accessed | tf_op | source)
XLA Modules:
  0.0 288.1 jit_solution(18204161635696154360)
XLA Ops:
  7.9 45.3 %all_gather.3 = bf16[32,8192]{1,0:T(8,128)(2,1)S(1)} all-gather(bf16[32,512]{1,0:T(8,128)(2,1)S(1)} %pad_maximum_fusion), channel_id=1, replica_groups=mesh['feat'=16,'rows'=2] {'feat'}, dimensions={1}, use_global_device_ids=true | all-gather | bytes 557056 | tf_op jit(solution)/shard_map/all_gather | solution.py:56
  53.3 155.4 %while.14 = (s32[]{:T(128)}, f32[32,8192]{1,0:T(8,128)S(1)}, bf16[32,8192]{1,0:T(8,128)(2,1)S(1)}, s32[32,8192]{1,0:T(8,128)}, s32[]{:T(128)}, /*index=5*/s32[]{:T(128)}, s32[]{:T(128)}, s32[]{:T(128)}) while((s32[]{:T(128)}, f32[32,8192]{1,0:T(8,128)S(1)}, bf16[32,8192]{1,0:T(8,128)(2,1)S(1)}, s32[32,8192]{1,0:T(8,128)}, ...), condition=%wide.region_1.0_spmd.clone, body=%wide.region_0.0_spmd.clone.sunk | while | flops 273154048 | bytes 10846365 | solution.py:49
  58.1 4.8 %convolution_add_fusion.2 = f32[32,8192]{1,0:T(8,128)S(1)} fusion(pred[8192,512]{1,0:T(32,128)(4,1)} %bitcast_compare_fusion.2, f32[32,8192]{1,0:T(8,128)S(1)} %get-tuple-element.148, pred[]{:T(512)S(6)} %compare.3, bf16[32,8192]{1,0:T(8,128)(2,1)S(1)} %get-tuple-element.157, s32[]{:T(128)S(6)} %select_n.14), kind=kOutput, calls=%fused_computation.1.clone.1 | convolution fusion | flops 268959744 | bytes 6324229 | tf_op jit(solution)/shard_map/while/body/eval_jaxpr/dot_general | solution.py:35
  67.9 4.8 %convolution_add_fusion.2 = f32[32,8192]{1,0:T(8,128)S(1)} fusion(pred[8192,512]{1,0:T(32,128)(4,1)} %bitcast_compare_fusion.2, f32[32,8192]{1,0:T(8,128)S(1)} %get-tuple-element.148, pred[]{:T(512)S(6)} %compare.3, bf16[32,8192]{1,0:T(8,128)(2,1)S(1)} %get-tuple-element.157, s32[]{:T(128)S(6)} %select_n.14), kind=kOutput, calls=%fused_computation.1.clone.1 | convolution fusion | flops 268959744 | bytes 6324229 | tf_op jit(solution)/shard_map/while/body/eval_jaxpr/dot_general | solution.py:35
  73.6 4.0 %bitcast_compare_fusion.2 = pred[8192,512]{1,0:T(32,128)(4,1)} fusion(s32[8192]{0:T(1024)S(1)} %bitcast.39, s32[32,512]{1,0:T(8,128)S(1)} %constant_dynamic-slice_fusion.5), kind=kLoop, calls=%fused_computation.clone.1 | loop fusion | flops 4194304 | bytes 4292608 | tf_op jit(solution)/shard_map/while/body/eval_jaxpr/eq | solution.py:34
  77.6 4.8 %convolution_add_fusion.2 = f32[32,8192]{1,0:T(8,128)S(1)} fusion(pred[8192,512]{1,0:T(32,128)(4,1)} %bitcast_compare_fusion.2, f32[32,8192]{1,0:T(8,128)S(1)} %get-tuple-element.148, pred[]{:T(512)S(6)} %compare.3, bf16[32,8192]{1,0:T(8,128)(2,1)S(1)} %get-tuple-element.157, s32[]{:T(128)S(6)} %select_n.14), kind=kOutput, calls=%fused_computation.1.clone.1 | convolution fusion | flops 268959744 | bytes 6324229 | tf_op jit(solution)/shard_map/while/body/eval_jaxpr/dot_general | solution.py:35
  83.3 4.0 %bitcast_compare_fusion.2 = pred[8192,512]{1,0:T(32,128)(4,1)} fusion(s32[8192]{0:T(1024)S(1)} %bitcast.39, s32[32,512]{1,0:T(8,128)S(1)} %constant_dynamic-slice_fusion.5), kind=kLoop, calls=%fused_computation.clone.1 | loop fusion | flops 4194304 | bytes 4292608 | tf_op jit(solution)/shard_map/while/body/eval_jaxpr/eq | solution.py:34
  87.3 4.8 %convolution_add_fusion.2 = f32[32,8192]{1,0:T(8,128)S(1)} fusion(pred[8192,512]{1,0:T(32,128)(4,1)} %bitcast_compare_fusion.2, f32[32,8192]{1,0:T(8,128)S(1)} %get-tuple-element.148, pred[]{:T(512)S(6)} %compare.3, bf16[32,8192]{1,0:T(8,128)(2,1)S(1)} %get-tuple-element.157, s32[]{:T(128)S(6)} %select_n.14), kind=kOutput, calls=%fused_computation.1.clone.1 | convolution fusion | flops 268959744 | bytes 6324229 | tf_op jit(solution)/shard_map/while/body/eval_jaxpr/dot_general | solution.py:35
  97.0 4.8 %convolution_add_fusion.2 = f32[32,8192]{1,0:T(8,128)S(1)} fusion(pred[8192,512]{1,0:T(32,128)(4,1)} %bitcast_compare_fusion.2, f32[32,8192]{1,0:T(8,128)S(1)} %get-tuple-element.148, pred[]{:T(512)S(6)} %compare.3, bf16[32,8192]{1,0:T(8,128)(2,1)S(1)} %get-tuple-element.157, s32[]{:T(128)S(6)} %select_n.14), kind=kOutput, calls=%fused_computation.1.clone.1 | convolution fusion | flops 268959744 | bytes 6324229 | tf_op jit(solution)/shard_map/while/body/eval_jaxpr/dot_general | solution.py:35
  106.7 4.8 %convolution_add_fusion.2 = f32[32,8192]{1,0:T(8,128)S(1)} fusion(pred[8192,512]{1,0:T(32,128)(4,1)} %bitcast_compare_fusion.2, f32[32,8192]{1,0:T(8,128)S(1)} %get-tuple-element.148, pred[]{:T(512)S(6)} %compare.3, bf16[32,8192]{1,0:T(8,128)(2,1)S(1)} %get-tuple-element.157, s32[]{:T(128)S(6)} %select_n.14), kind=kOutput, calls=%fused_computation.1.clone.1 | convolution fusion | flops 268959744 | bytes 6324229 | tf_op jit(solution)/shard_map/while/body/eval_jaxpr/dot_general | solution.py:35
  116.4 4.8 %convolution_add_fusion.2 = f32[32,8192]{1,0:T(8,128)S(1)} fusion(pred[8192,512]{1,0:T(32,128)(4,1)} %bitcast_compare_fusion.2, f32[32,8192]{1,0:T(8,128)S(1)} %get-tuple-element.148, pred[]{:T(512)S(6)} %compare.3, bf16[32,8192]{1,0:T(8,128)(2,1)S(1)} %get-tuple-element.157, s32[]{:T(128)S(6)} %select_n.14), kind=kOutput, calls=%fused_computation.1.clone.1 | convolution fusion | flops 268959744 | bytes 6324229 | tf_op jit(solution)/shard_map/while/body/eval_jaxpr/dot_general | solution.py:35
  126.1 4.8 %convolution_add_fusion.2 = f32[32,8192]{1,0:T(8,128)S(1)} fusion(pred[8192,512]{1,0:T(32,128)(4,1)} %bitcast_compare_fusion.2, f32[32,8192]{1,0:T(8,128)S(1)} %get-tuple-element.148, pred[]{:T(512)S(6)} %compare.3, bf16[32,8192]{1,0:T(8,128)(2,1)S(1)} %get-tuple-element.157, s32[]{:T(128)S(6)} %select_n.14), kind=kOutput, calls=%fused_computation.1.clone.1 | convolution fusion | flops 268959744 | bytes 6324229 | tf_op jit(solution)/shard_map/while/body/eval_jaxpr/dot_general | solution.py:35
  135.8 4.8 %convolution_add_fusion.2 = f32[32,8192]{1,0:T(8,128)S(1)} fusion(pred[8192,512]{1,0:T(32,128)(4,1)} %bitcast_compare_fusion.2, f32[32,8192]{1,0:T(8,128)S(1)} %get-tuple-element.148, pred[]{:T(512)S(6)} %compare.3, bf16[32,8192]{1,0:T(8,128)(2,1)S(1)} %get-tuple-element.157, s32[]{:T(128)S(6)} %select_n.14), kind=kOutput, calls=%fused_computation.1.clone.1 | convolution fusion | flops 268959744 | bytes 6324229 | tf_op jit(solution)/shard_map/while/body/eval_jaxpr/dot_general | solution.py:35
  145.6 4.8 %convolution_add_fusion.2 = f32[32,8192]{1,0:T(8,128)S(1)} fusion(pred[8192,512]{1,0:T(32,128)(4,1)} %bitcast_compare_fusion.2, f32[32,8192]{1,0:T(8,128)S(1)} %get-tuple-element.148, pred[]{:T(512)S(6)} %compare.3, bf16[32,8192]{1,0:T(8,128)(2,1)S(1)} %get-tuple-element.157, s32[]{:T(128)S(6)} %select_n.14), kind=kOutput, calls=%fused_computation.1.clone.1 | convolution fusion | flops 268959744 | bytes 6324229 | tf_op jit(solution)/shard_map/while/body/eval_jaxpr/dot_general | solution.py:35
  155.3 4.8 %convolution_add_fusion.2 = f32[32,8192]{1,0:T(8,128)S(1)} fusion(pred[8192,512]{1,0:T(32,128)(4,1)} %bitcast_compare_fusion.2, f32[32,8192]{1,0:T(8,128)S(1)} %get-tuple-element.148, pred[]{:T(512)S(6)} %compare.3, bf16[32,8192]{1,0:T(8,128)(2,1)S(1)} %get-tuple-element.157, s32[]{:T(128)S(6)} %select_n.14), kind=kOutput, calls=%fused_computation.1.clone.1 | convolution fusion | flops 268959744 | bytes 6324229 | tf_op jit(solution)/shard_map/while/body/eval_jaxpr/dot_general | solution.py:35
  165.0 4.8 %convolution_add_fusion.2 = f32[32,8192]{1,0:T(8,128)S(1)} fusion(pred[8192,512]{1,0:T(32,128)(4,1)} %bitcast_compare_fusion.2, f32[32,8192]{1,0:T(8,128)S(1)} %get-tuple-element.148, pred[]{:T(512)S(6)} %compare.3, bf16[32,8192]{1,0:T(8,128)(2,1)S(1)} %get-tuple-element.157, s32[]{:T(128)S(6)} %select_n.14), kind=kOutput, calls=%fused_computation.1.clone.1 | convolution fusion | flops 268959744 | bytes 6324229 | tf_op jit(solution)/shard_map/while/body/eval_jaxpr/dot_general | solution.py:35
  174.7 4.8 %convolution_add_fusion.2 = f32[32,8192]{1,0:T(8,128)S(1)} fusion(pred[8192,512]{1,0:T(32,128)(4,1)} %bitcast_compare_fusion.2, f32[32,8192]{1,0:T(8,128)S(1)} %get-tuple-element.148, pred[]{:T(512)S(6)} %compare.3, bf16[32,8192]{1,0:T(8,128)(2,1)S(1)} %get-tuple-element.157, s32[]{:T(128)S(6)} %select_n.14), kind=kOutput, calls=%fused_computation.1.clone.1 | convolution fusion | flops 268959744 | bytes 6324229 | tf_op jit(solution)/shard_map/while/body/eval_jaxpr/dot_general | solution.py:35
  184.4 4.8 %convolution_add_fusion.2 = f32[32,8192]{1,0:T(8,128)S(1)} fusion(pred[8192,512]{1,0:T(32,128)(4,1)} %bitcast_compare_fusion.2, f32[32,8192]{1,0:T(8,128)S(1)} %get-tuple-element.148, pred[]{:T(512)S(6)} %compare.3, bf16[32,8192]{1,0:T(8,128)(2,1)S(1)} %get-tuple-element.157, s32[]{:T(128)S(6)} %select_n.14), kind=kOutput, calls=%fused_computation.1.clone.1 | convolution fusion | flops 268959744 | bytes 6324229 | tf_op jit(solution)/shard_map/while/body/eval_jaxpr/dot_general | solution.py:35
  194.1 4.8 %convolution_add_fusion.2 = f32[32,8192]{1,0:T(8,128)S(1)} fusion(pred[8192,512]{1,0:T(32,128)(4,1)} %bitcast_compare_fusion.2, f32[32,8192]{1,0:T(8,128)S(1)} %get-tuple-element.148, pred[]{:T(512)S(6)} %compare.3, bf16[32,8192]{1,0:T(8,128)(2,1)S(1)} %get-tuple-element.157, s32[]{:T(128)S(6)} %select_n.14), kind=kOutput, calls=%fused_computation.1.clone.1 | convolution fusion | flops 268959744 | bytes 6324229 | tf_op jit(solution)/shard_map/while/body/eval_jaxpr/dot_general | solution.py:35
  203.8 4.8 %convolution_add_fusion.2 = f32[32,8192]{1,0:T(8,128)S(1)} fusion(pred[8192,512]{1,0:T(32,128)(4,1)} %bitcast_compare_fusion.2, f32[32,8192]{1,0:T(8,128)S(1)} %get-tuple-element.148, pred[]{:T(512)S(6)} %compare.3, bf16[32,8192]{1,0:T(8,128)(2,1)S(1)} %get-tuple-element.157, s32[]{:T(128)S(6)} %select_n.14), kind=kOutput, calls=%fused_computation.1.clone.1 | convolution fusion | flops 268959744 | bytes 6324229 | tf_op jit(solution)/shard_map/while/body/eval_jaxpr/dot_general | solution.py:35
  210.0 15.4 %all-reduce.2.cloned.1.call-done = f32[2,16,32,256]{3,2,1,0:T(8,128)} async-done(((f32[2,16,32,256]{3,2,1,0:T(8,128)}), f32[2,16,32,256]{3,2,1,0:T(8,128)}) %all-reduce.2.cloned.1.call-update) | async-done | bytes 1048592 | tf_op jit(solution)/shard_map/psum | solution.py:59
  227.0 4.6 %reduce-window.16 = f32[8,32,2,128]{3,1,2,0:T(8,128)S(1)} reduce-window(f32[8,32,2,128]{3,1,2,0:T(8,128)S(1)} %copy.19, f32[]{:T(128)} %constant.45.clone.1), window={size=1x1x1x128 pad=0_0x0_0x0_0x127_0}, to_apply=%region_5.6 | reduce-window | flops 8323072 | bytes 524292 | tf_op jit(solution)/shard_map/reduce-window.2
  231.6 4.6 %reduce-window.14 = f32[8,32,2,128]{3,1,2,0:T(8,128)S(1)} reduce-window(f32[8,32,2,128]{3,1,2,0:T(8,128)S(1)} %copy.16, f32[]{:T(128)} %constant.45.clone.1), window={size=1x1x1x128 pad=0_0x0_0x0_0x127_0}, to_apply=%region_3.0 | reduce-window | flops 8323072 | bytes 524292 | tf_op jit(solution)/shard_map/reduce-window
  237.9 42.5 %pmax.7 = f32[8]{0:T(128)} all-reduce(f32[8]{0:T(128)S(1)} %subtract_reduce_fusion), channel_id=1, replica_groups=mesh['feat'=16,'rows'=2] {'feat'}, use_global_device_ids=true, to_apply=%region_8.9 | all-reduce | flops 8 | bytes 64 | tf_op jit(solution)/shard_map/pmax | solution.py:61
  (89 shorter events, 75.8 us)
Async XLA Ops:
  7.2 218.3 %all-reduce.2.cloned.1.call-start = ((), (), s32[]{:S(2)}) async-start(), calls=%async_computation | async-start | bytes 2097152 | tf_op jit(solution)/shard_map/psum | solution.py:59
  225.5 54.9 %copy-start = (f32[2,16,32,256]{3,2,1,0:T(8,128)S(1)}, f32[2,16,32,256]{3,2,1,0:T(8,128)}, u32[]{:S(2)}) copy-start(f32[2,16,32,256]{3,2,1,0:T(8,128)} %all-reduce.2.cloned.1.call-done) | copy-start | bytes 3145732
Sparse Core Ops, SparseCore 0:
  210.2 15.2 all-reduce.1
where the time goes:
time: 290 us; the launch traced here: 288 us
  blocking collectives  87.8 us (30%)
  matrix products  76.9 us (27%)
  other arithmetic  74.7 us (26%)
  local copies, waits for them, and re-layouts  18.2 us (6%)
  waiting for transfers between devices  15.4 us (5%)
  between operations  14.2 us (5%)
    dot_general x16, matrix products, add_block(): lax.dot_general(panel_block, one_hot, (((1,), (1,)), ((), ())), preferred...  76.9 us
    eq x16, other arithmetic, add_block(): bins_block[:, None, :] == bin_ids  63.8 us
    all_gather x1, blocking collectives, local(): lax.all_gather(local_panel, 'feat', axis=1, tiled=True)  45.3 us
    pmax x1, blocking collectives, local(): best = lax.pmax(split_gain(mine), 'feat')  42.5 us
    psum x1, waiting for transfers between devices, local(): total = lax.psum(hist, 'rows')  15.4 us
    dynamic_slice x16, local copies, waits for them, and re-layouts, step(): bins_block = lax.dynamic_slice_in_dim(bins_part, begin, block_rows, 1)  13.6 us
    another operation x5, other arithmetic  9.56 us
  transfers between devices with their start and end apart: 1, of which 1 were waited for; matrix products, arithmetic and copies ran while one was open for 0% of the time, Pallas kernels for 0%

commit v1 on v0

v1 whole, which is shorter than its diff:
```python
import functools

import jax
import jax.numpy as jnp
from jax import lax
from jax.experimental import pallas as pl
from jax.experimental.pallas import tpu as pltpu
from jax.sharding import PartitionSpec as P

BINS = 256
NODES = 16
LO = 128
HI = BINS // LO
PANEL = 2 * NODES
CHUNK = 2048

reg_lambda = 1.0


def build_panel(gathered, panel, slot, count):
    g = gathered[slot, 0:1, :].astype(jnp.float32)
    h = gathered[slot, 1:2, :].astype(jnp.float32)
    n = gathered[slot, 2:3, :].astype(jnp.float32)
    row = lax.broadcasted_iota(jnp.int32, (PANEL, count), 0)
    value = jnp.where(row % 2 == 0, jnp.broadcast_to(g, row.shape), jnp.broadcast_to(h, row.shape))
    hit = jnp.broadcast_to(n, row.shape) == (row // 2).astype(jnp.float32)
    begin = pl.multiple_of(slot * count, count)
    panel[:, pl.ds(begin, count)] = jnp.where(hit, value, 0.0).astype(jnp.bfloat16)


def one_feature(bins_v, panel, acc, f, feats, chunk):
    rows = bins_v.shape[1]
    total = jnp.zeros((HI * PANEL, LO), jnp.float32)
    base = lax.broadcasted_iota(jnp.int32, (LO // 16, 16, 128), 0) * 16
    ids = (base + lax.broadcasted_iota(jnp.int32, base.shape, 1)).astype(jnp.float32).astype(jnp.bfloat16)
    ids = jnp.concatenate([ids] * (chunk // 128), axis=2)
    for begin in range(0, rows, chunk):
        x = bins_v[pl.ds(f, 1), begin : begin + chunk]
        x = jnp.broadcast_to(x, (16, chunk)).astype(jnp.float32).astype(jnp.bfloat16)
        high = x >= jnp.bfloat16(LO)
        low = jnp.where(high, x - jnp.bfloat16(LO), x)
        part = panel[:, begin : begin + chunk].reshape(PANEL // 16, 16, chunk)
        zero = jnp.zeros_like(part)
        high3 = jnp.broadcast_to(high[None], part.shape)
        left = jnp.concatenate([jnp.where(high3, zero, part), jnp.where(high3, part, zero)], axis=0)
        left = left.reshape(HI * PANEL, chunk)
        hot = jnp.broadcast_to(low[None], ids.shape) == ids
        hot = jnp.where(hot, jnp.ones(ids.shape, jnp.bfloat16), jnp.zeros(ids.shape, jnp.bfloat16))
        hot = hot.reshape(LO, chunk)
        total = total + lax.dot_general(
            left, hot, (((1,), (1,)), ((), ())), preferred_element_type=jnp.float32
        )
    for hi in range(HI):
        acc[hi, pl.ds(f, PANEL, stride=feats), :] = total[hi * PANEL : (hi + 1) * PANEL]


def kernel(
    n_feat, n_rows, pack, bins, hist, best,
    bins_v, gathered, panel, acc, inbox, mine_max, max_in,
    bins_sem, own_sem, ag_send, ag_recv, ex_send, ex_recv, mx_send, mx_recv,
):
    me = lax.axis_index("feat")
    my_row = lax.axis_index("rows")
    feats = bins_v.shape[0]
    count = pack.shape[1]
    share = NODES // n_rows
    span = share * 2 * feats

    load = pltpu.make_async_copy(bins, bins_v, bins_sem)
    load.start()

    barrier = pltpu.get_barrier_semaphore()
    for step in range(1, n_feat):
        pl.semaphore_signal(barrier, inc=1, device_id={"feat": lax.rem(me + step, n_feat)})
    for step in range(1, n_rows):
        pl.semaphore_signal(barrier, inc=1, device_id={"rows": lax.rem(my_row + step, n_rows)})
    pl.semaphore_wait(barrier, n_feat + n_rows - 2)

    def ag_copy(step):
        return pltpu.make_async_remote_copy(
            src_ref=pack,
            dst_ref=gathered.at[me],
            send_sem=ag_send.at[step],
            recv_sem=ag_recv.at[step],
            device_id={"feat": lax.rem(me + step, n_feat)},
        )

    for step in range(1, n_feat):
        ag_copy(step).start()
    own = pltpu.make_async_copy(pack, gathered.at[me], own_sem)
    own.start()
    own.wait()
    for step in range(1, n_feat):
        ag_copy(step).wait()
    load.wait()

    @pl.loop(0, n_feat)
    def _(slot):
        build_panel(gathered, panel, slot, count)

    @pl.loop(0, feats)
    def _(f):
        one_feature(bins_v, panel, acc, f, feats, min(CHUNK, bins_v.shape[1]))

    def ex_copy(step):
        target = lax.rem(my_row + step, n_rows)
        return pltpu.make_async_remote_copy(
            src_ref=acc.at[:, pl.ds(pl.multiple_of(target * span, span), span), :],
            dst_ref=inbox.at[step - 1],
            send_sem=ex_send.at[step],
            recv_sem=ex_recv.at[step],
            device_id={"rows": target},
        )

    for step in range(1, n_rows):
        ex_copy(step).start()
    for step in range(1, n_rows):
        ex_copy(step).wait()

    begin = pl.multiple_of(my_row * span, span)
    tri_in = lax.broadcasted_iota(jnp.int32, (LO, LO), 0)
    tri_out = lax.broadcasted_iota(jnp.int32, (LO, LO), 1)
    tri = (tri_in <= tri_out).astype(jnp.float32)
    lefts = []
    base = None
    for hi in range(HI):
        mine = acc[hi, pl.ds(begin, span), :]
        for step in range(1, n_rows):
            mine = mine + inbox[step - 1, hi]
        for n in range(share):
            for c in range(2):
                at = (n * 2 + c) * feats
                hist[c, n, :, hi * LO : (hi + 1) * LO] = mine[at : at + feats]
        left = lax.dot_general(
            mine, tri, (((1,), (0,)), ((), ())),
            precision=lax.Precision.HIGHEST, preferred_element_type=jnp.float32,
        )
        if base is not None:
            left = left + base
        base = left[:, LO - 1 : LO]
        lefts.append(left.reshape(share, 2, feats, LO))
    whole = base.reshape(share, 2, feats, 1)
    total_g, total_h = whole[:, 0], whole[:, 1]
    top = None
    for left in lefts:
        left_g, left_h = left[:, 0], left[:, 1]
        gain = left_g * left_g / (left_h + reg_lambda)
        gain = gain + (total_g - left_g) ** 2 / (total_h - left_h + reg_lambda)
        gain = gain - total_g * total_g / (total_h + reg_lambda)
        gain = jnp.max(gain, axis=1)
        top = gain if top is None else jnp.maximum(top, gain)
    mine_max[...] = top

    def mx_copy(step):
        return pltpu.make_async_remote_copy(
            src_ref=mine_max,
            dst_ref=max_in.at[step - 1],
            send_sem=mx_send.at[step],
            recv_sem=mx_recv.at[step],
            device_id={"feat": lax.rem(me + step, n_feat)},
        )

    for step in range(1, n_feat):
        mx_copy(step).start()
    for step in range(1, n_feat):
        mx_copy(step).wait()
    for step in range(1, n_feat):
        top = jnp.maximum(top, max_in[step - 1])
    best[...] = jnp.broadcast_to(jnp.max(top, axis=1, keepdims=True), best.shape)


def local(n_feat, n_rows, grads, hessians, nodes, bins):
    feats, rows = bins.shape
    count = grads.shape[0]
    share = NODES // n_rows
    span = share * 2 * feats
    pack = jnp.stack([grads, hessians, nodes.astype(jnp.bfloat16), jnp.zeros_like(grads)])
    vmem = pl.BlockSpec(memory_space=pltpu.VMEM)
    hist, best = pl.pallas_call(
        functools.partial(kernel, n_feat, n_rows),
        out_shape=(
            jax.ShapeDtypeStruct((2, share, feats, BINS), jnp.float32),
            jax.ShapeDtypeStruct((share, 128), jnp.float32),
        ),
        in_specs=[vmem, pl.BlockSpec(memory_space=pl.ANY)],
        out_specs=(vmem, vmem),
        scratch_shapes=[
            pltpu.VMEM((feats, rows), jnp.int32),
            pltpu.VMEM((n_feat, 4, count), jnp.bfloat16),
            pltpu.VMEM((PANEL, rows), jnp.bfloat16),
            pltpu.VMEM((HI, PANEL * feats, LO), jnp.float32),
            pltpu.VMEM((max(n_rows - 1, 1), HI, span, LO), jnp.float32),
            pltpu.VMEM((share, LO), jnp.float32),
            pltpu.VMEM((max(n_feat - 1, 1), share, LO), jnp.float32),
            pltpu.SemaphoreType.DMA,
            pltpu.SemaphoreType.DMA,
            pltpu.SemaphoreType.DMA((n_feat,)),
            pltpu.SemaphoreType.DMA((n_feat,)),
            pltpu.SemaphoreType.DMA((n_rows,)),
            pltpu.SemaphoreType.DMA((n_rows,)),
            pltpu.SemaphoreType.DMA((n_feat,)),
            pltpu.SemaphoreType.DMA((n_feat,)),
        ],
        compiler_params=pltpu.CompilerParams(
            collective_id=0, has_side_effects=True, vmem_limit_bytes=56 << 20
        ),
        name="tree_level",
    )(pack, bins)
    return hist, best[:, 0]


def solution(mesh):
    return jax.shard_map(
        functools.partial(local, mesh.shape["feat"], mesh.shape["rows"]),
        mesh=mesh,
        in_specs=(P(("rows", "feat")), P(("rows", "feat")), P(("rows", "feat")), P("feat", "rows")),
        out_specs=(P(None, "rows", "feat", None), P("rows")),
        check_vma=False,
    )
```

time: 290 us -> 55.5 us (0.19)
  blocking collectives: 87.8 us -> 0 us
  matrix products: 76.9 us -> 0 us
  other arithmetic: 74.7 us -> 0.67 us
  Pallas kernels: 0 us -> 48.7 us
  waiting for transfers between devices: 15.4 us -> 0 us
  between operations: 14.2 us -> 0.65 us
  local copies, waits for them, and re-layouts: 18.2 us -> 5.22 us
    dot_general x16 -> x0, matrix products: 76.9 us -> none  [add_block(): lax.dot_general(panel_block, one_hot, (((1,), (1,)), ((), ())), preferred...]
    eq x16 -> x0, other arithmetic: 63.8 us -> none  [add_block(): bins_block[:, None, :] == bin_ids]
    pallas_call x0 -> x1, Pallas kernels: none -> 48.7 us  [local(): pl.pallas_call(functools.partial(kernel, n_feat, n_rows), out_shape=(jax....]
    all_gather x1 -> x0, blocking collectives: 45.3 us -> none  [local(): lax.all_gather(local_panel, 'feat', axis=1, tiled=True)]
    pmax x1 -> x0, blocking collectives: 42.5 us -> none  [local(): best = lax.pmax(split_gain(mine), 'feat')]
    psum x1 -> x0, waiting for transfers between devices: 15.4 us -> none  [local(): total = lax.psum(hist, 'rows')]
    dynamic_slice x17 -> x0, local copies, waits for them, and re-layouts: 14.4 us -> none  [the longest x16 13.6 us: step(): bins_block = lax.dynamic_slice_in_dim(bins_part, begin, block_rows, 1)]
    another operation x5 -> x1, other arithmetic: 9.56 us -> 0.66 us  [local(): jnp.stack([grads, hessians, nodes.astype(jnp.bfloat16), jnp.zeros_like(gr...]
  transfers between devices with their start and end apart: 1 -> 0, of which waited for: 1 -> 0; matrix products, arithmetic and copies ran while one was open for 0% -> 0% of each run, Pallas kernels for 0% -> 0%
where the time goes in v1:
time: 55.5 us; the launch traced here: 55.2 us
  Pallas kernels  48.7 us (88%)
  local copies, waits for them, and re-layouts  5.22 us (9%)
  other arithmetic  0.67 us (1%)
  between operations  0.65 us (1%)
    pallas_call x1, Pallas kernels, local(): pl.pallas_call(functools.partial(kernel, n_feat, n_rows), out_shape=(jax....  48.7 us
    unnamed x7, local copies, waits for them, and re-layouts  3.82 us
    slice x1, local copies, waits for them, and re-layouts, local(): return (hist, best[:, 0])  1.31 us

profile of v1, /device:TPU:0, one launch (start us, length us, event | category | flops | bytes accessed | tf_op | source)
XLA Modules:
  0.0 55.2 jit_solution(5324591129565794841)
XLA Ops:
  0.6 0.0 copy-start
  0.6 0.1 pad.3.clone
  0.7 0.6 %copy-done = s32[512]{0:T(512)S(1)} copy-done((s32[512]{0:T(512)S(1)}, s32[512]{0:T(512)}, u32[]{:S(2)}) %copy-start) | copy-done | bytes 2072
  1.3 0.0 copy-start.1
  1.3 0.7 %copy-done.1 = bf16[512]{0:T(512)(128)(2,1)S(1)} copy-done((bf16[512]{0:T(512)(128)(2,1)S(1)}, bf16[512]{0:T(512)(128)(2,1)}, u32[]{:S(2)}) %copy-start.1) | copy-done | bytes 1048
  2.0 0.0 copy-start.2
  2.0 0.7 %copy-done.2 = bf16[512]{0:T(512)(128)(2,1)S(1)} copy-done((bf16[512]{0:T(512)(128)(2,1)S(1)}, bf16[512]{0:T(512)(128)(2,1)}, u32[]{:S(2)}) %copy-start.2) | copy-done | bytes 1048
  2.7 0.7 %maximum_maximum_fusion.pack = bf16[4,512]{1,0:T(4,128)(2,1)} fusion(bf16[1,512]{1,0:T(2,128)(2,1)S(1)} %stack.14, bf16[1,512]{1,0:T(2,128)(2,1)S(1)} %stack.13, bf16[1,512]{1,0:T(2,128)(2,1)S(1)} %stack.12, bf16[4]{0:T(256)(128)(2,1)S(1)} %pad.3.clone), kind=kLoop, calls=%fused_computation | loop fusion | flops 16384 | bytes 7176 | tf_op jit(solution)/shard_map/stack | solution.py:177
  3.3 48.7 %tree_level.1 = (f32[2,8,32,256]{3,2,1,0:T(8,128)}, f32[8,128]{1,0:T(8,128)}) custom-call(bf16[4,512]{1,0:T(4,128)(2,1)} %maximum_maximum_fusion.pack, s32[32,8192]{1,0:T(8,128)} %bins.1), custom_call_target="tpu_custom_call" | custom-call | tf_op jit(solution)/shard_map/tree_level/pallas_call | solution.py:179
  52.0 1.3 %slice_reduce_fusion = f32[8]{0:T(128)} fusion(f32[8,128]{1,0:T(8,128)} %get-tuple-element.5), kind=kLoop, calls=%fused_computation.1 | loop fusion | bytes 64 | tf_op jit(solution)/shard_map/slice | solution.py:209
  53.4 1.9 %copy.7 = f32[2,8,32,256]{3,2,1,0:T(8,128)} copy(f32[2,8,32,256]{3,2,1,0:T(8,128)} %get-tuple-element.8) | data formatting | bytes 1048576
  (4 shorter events, 0.0 us)
Async XLA Ops:
  0.6 0.7 %copy-start = (s32[512]{0:T(512)S(1)}, s32[512]{0:T(512)}, u32[]{:S(2)}) copy-start(s32[512]{0:T(512)} %param.6) | copy-start | bytes 6148
  1.3 0.7 %copy-start.1 = (bf16[512]{0:T(512)(128)(2,1)S(1)}, bf16[512]{0:T(512)(128)(2,1)}, u32[]{:S(2)}) copy-start(bf16[512]{0:T(512)(128)(2,1)} %param.4) | copy-start | bytes 3076
  2.0 0.7 %copy-start.2 = (bf16[512]{0:T(512)(128)(2,1)S(1)}, bf16[512]{0:T(512)(128)(2,1)}, u32[]{:S(2)}) copy-start(bf16[512]{0:T(512)(128)(2,1)} %param.5) | copy-start | bytes 3076

commit v2 on v1

--- a/solution.py
+++ b/solution.py
@@ -12,7 +12,8 @@
 LO = 128
 HI = BINS // LO
 PANEL = 2 * NODES
-CHUNK = 2048
+CHUNK = 1024
+UNROLL = 4
 
 reg_lambda = 1.0
 
@@ -30,7 +31,7 @@
 
 def one_feature(bins_v, panel, acc, f, feats, chunk):
     rows = bins_v.shape[1]
-    total = jnp.zeros((HI * PANEL, LO), jnp.float32)
+    total = jnp.zeros((LO, HI * PANEL), jnp.float32)
     base = lax.broadcasted_iota(jnp.int32, (LO // 16, 16, 128), 0) * 16
     ids = (base + lax.broadcasted_iota(jnp.int32, base.shape, 1)).astype(jnp.float32).astype(jnp.bfloat16)
     ids = jnp.concatenate([ids] * (chunk // 128), axis=2)
@@ -48,8 +49,9 @@
         hot = jnp.where(hot, jnp.ones(ids.shape, jnp.bfloat16), jnp.zeros(ids.shape, jnp.bfloat16))
         hot = hot.reshape(LO, chunk)
         total = total + lax.dot_general(
-            left, hot, (((1,), (1,)), ((), ())), preferred_element_type=jnp.float32
-        )
+            hot, left, (((1,), (1,)), ((), ())), preferred_element_type=jnp.float32
+        )
+    total = total.T
     for hi in range(HI):
         acc[hi, pl.ds(f, PANEL, stride=feats), :] = total[hi * PANEL : (hi + 1) * PANEL]
 
@@ -98,9 +100,10 @@
     def _(slot):
         build_panel(gathered, panel, slot, count)
 
-    @pl.loop(0, feats)
-    def _(f):
-        one_feature(bins_v, panel, acc, f, feats, min(CHUNK, bins_v.shape[1]))
+    @pl.loop(0, feats // UNROLL)
+    def _(group):
+        for at in range(UNROLL):
+            one_feature(bins_v, panel, acc, group * UNROLL + at, feats, min(CHUNK, bins_v.shape[1]))
 
     def ex_copy(step):
         target = lax.rem(my_row + step, n_rows)

time: 55.5 us -> 47.2 us (0.85)
  Pallas kernels: 48.7 us -> 40.4 us
    pallas_call x1, Pallas kernels: 48.7 us -> 40.4 us  [local(): pl.pallas_call(functools.partial(kernel, n_feat, n_rows), out_shape=(jax....]
where the time goes in v2:
time: 47.2 us; the launch traced here: 46.9 us
  Pallas kernels  40.4 us (86%)
  local copies, waits for them, and re-layouts  5.22 us (11%)
  other arithmetic  0.67 us (1%)
  between operations  0.65 us (1%)
    pallas_call x1, Pallas kernels, local(): pl.pallas_call(functools.partial(kernel, n_feat, n_rows), out_shape=(jax....  40.4 us
    unnamed x7, local copies, waits for them, and re-layouts  3.82 us
    slice x1, local copies, waits for them, and re-layouts, local(): return (hist, best[:, 0])  1.31 us

profile of v2, /device:TPU:0, one launch (start us, length us, event | category | flops | bytes accessed | tf_op | source)
XLA Modules:
  0.0 46.9 jit_solution(8156353966199099216)
XLA Ops:
  0.6 0.0 copy-start
  0.6 0.1 pad.3.clone
  0.7 0.6 %copy-done = s32[512]{0:T(512)S(1)} copy-done((s32[512]{0:T(512)S(1)}, s32[512]{0:T(512)}, u32[]{:S(2)}) %copy-start) | copy-done | bytes 2072
  1.3 0.0 copy-start.1
  1.3 0.7 %copy-done.1 = bf16[512]{0:T(512)(128)(2,1)S(1)} copy-done((bf16[512]{0:T(512)(128)(2,1)S(1)}, bf16[512]{0:T(512)(128)(2,1)}, u32[]{:S(2)}) %copy-start.1) | copy-done | bytes 1048
  2.0 0.0 copy-start.2
  2.0 0.7 %copy-done.2 = bf16[512]{0:T(512)(128)(2,1)S(1)} copy-done((bf16[512]{0:T(512)(128)(2,1)S(1)}, bf16[512]{0:T(512)(128)(2,1)}, u32[]{:S(2)}) %copy-start.2) | copy-done | bytes 1048
  2.7 0.7 %maximum_maximum_fusion.pack = bf16[4,512]{1,0:T(4,128)(2,1)} fusion(bf16[1,512]{1,0:T(2,128)(2,1)S(1)} %stack.14, bf16[1,512]{1,0:T(2,128)(2,1)S(1)} %stack.13, bf16[1,512]{1,0:T(2,128)(2,1)S(1)} %stack.12, bf16[4]{0:T(256)(128)(2,1)S(1)} %pad.3.clone), kind=kLoop, calls=%fused_computation | loop fusion | flops 16384 | bytes 7176 | tf_op jit(solution)/shard_map/stack | solution.py:180
  3.3 40.4 %tree_level.1 = (f32[2,8,32,256]{3,2,1,0:T(8,128)}, f32[8,128]{1,0:T(8,128)}) custom-call(bf16[4,512]{1,0:T(4,128)(2,1)} %maximum_maximum_fusion.pack, s32[32,8192]{1,0:T(8,128)} %bins.1), custom_call_target="tpu_custom_call" | custom-call | tf_op jit(solution)/shard_map/tree_level/pallas_call | solution.py:182
  43.7 1.3 %slice_reduce_fusion = f32[8]{0:T(128)} fusion(f32[8,128]{1,0:T(8,128)} %get-tuple-element.5), kind=kLoop, calls=%fused_computation.1 | loop fusion | bytes 64 | tf_op jit(solution)/shard_map/slice | solution.py:212
  45.0 1.9 %copy.7 = f32[2,8,32,256]{3,2,1,0:T(8,128)} copy(f32[2,8,32,256]{3,2,1,0:T(8,128)} %get-tuple-element.8) | data formatting | bytes 1048576
  (4 shorter events, 0.0 us)
Async XLA Ops:
  0.6 0.7 %copy-start = (s32[512]{0:T(512)S(1)}, s32[512]{0:T(512)}, u32[]{:S(2)}) copy-start(s32[512]{0:T(512)} %param.6) | copy-start | bytes 6148
  1.3 0.7 %copy-start.1 = (bf16[512]{0:T(512)(128)(2,1)S(1)}, bf16[512]{0:T(512)(128)(2,1)}, u32[]{:S(2)}) copy-start(bf16[512]{0:T(512)(128)(2,1)} %param.4) | copy-start | bytes 3076
  2.0 0.7 %copy-start.2 = (bf16[512]{0:T(512)(128)(2,1)S(1)}, bf16[512]{0:T(512)(128)(2,1)}, u32[]{:S(2)}) copy-start(bf16[512]{0:T(512)(128)(2,1)} %param.5) | copy-start | bytes 3076
